TPU v7x, 32 devices: a whole 2x2x4 slice. The times are simulated.
32 devices in a mesh: expert: 8 (over z, y), dp: 4 (over x, core).
Axes of the slice: x: 2, y: 2, z: 4, core: 2. Of those that a mesh axis runs over, the one named last changes fastest.
Arguments:
- tokens: bfloat16 [4096, 1024], P(('expert', 'dp')), may hold values from -6 to 6
- routes: int32 [4096, 2], P(('expert', 'dp')), may hold values from 0 to 63, all different within a row; in each aligned block of 128 rows (0 to 127, 128 to 255, ...) at most 6 rows name the same one
- gate_values: float32 [4096, 2], P(('expert', 'dp')), may hold values from 0.02 to 0.5
- cotangent: bfloat16 [4096, 1024], P(('expert', 'dp')), may hold values from -6 to 6
- gating_weight: bfloat16 [64, 1024, 384], P('expert', 'dp'), may hold values from -0.1875 to 0.1875
- upward_weight: bfloat16 [64, 1024, 384], P('expert', 'dp'), may hold values from -0.1875 to 0.1875
- down_weight: bfloat16 [64, 1024, 384], P('expert', 'dp'), may hold values from -0.3125 to 0.3125
Outputs:
- layer_output: bfloat16 [4096, 1024], P(('expert', 'dp'))
- input_grad: bfloat16 [4096, 1024], P(('expert', 'dp'))
- gating_grad: float32 [64, 1024, 384], P('expert', 'dp')
- upward_grad: float32 [64, 1024, 384], P('expert', 'dp')
- down_grad: float32 [64, 1024, 384], P('expert', 'dp')
Inputs may be any that keep to these rules, and one draw needn't show every extreme that they name: `routes`: each row names 2 different experts. Among the rows of one device no expert is named more than 6 times, and in every draw some device names some expert exactly 6 times.
All inputs are finite; a program needn't handle non-finite values.
Results may differ from a plain program's by a relative error of at most 0.017.
Values may be sent and summed in bfloat16 or wider, within the bound.
A program may use at most 128 MiB of HBM per device.

v0:
```python
import functools
import jax
import jax.numpy as jnp
import numpy as np
from jax import lax
from jax.experimental import pallas as pl
from jax.experimental.pallas import tpu as pltpu
from jax.sharding import PartitionSpec as P

TOPK = 2
CAP = 6
MESH = pl.DeviceIdType.MESH
F32 = jnp.float32
BF16 = jnp.bfloat16


def plane_kernel(
    n_expert, n_dp, el, width,
    tok_ref, cot_ref, routes_ref, gates_ref, perm_ref, back_ref, wg_ref, wu_ref, wd_ref,
    layer_ref, igrad_ref, dg, du, dd,
    wg, wu, wd, halves, meta, send, recv, rows, psend, pown, crecv, xsend, xrecv, hid,
    pre_ret, ret_send, ret, fin_send, fin_recv,
    in_send, in_recv, out_send, out_recv, pair_sem, swap_sem, local_sem,
):
    e_me = lax.axis_index("expert")
    d_me = lax.axis_index("dp")
    z_me, y_me = e_me // 2, lax.rem(e_me, 2)
    zh_me, zl_me = z_me // 2, lax.rem(z_me, 2)
    x_me, c_me = d_me // 2, lax.rem(d_me, 2)
    n_zh = n_expert // 4
    core_peer = (e_me, x_me * 2 + 1 - c_me)
    far_peer = (e_me, (1 - x_me) * 2 + c_me)
    per = n_zh * n_dp
    msg = el * CAP
    part = per * CAP
    half = el // 2
    ff = wg.shape[2]
    row_count = tok_ref.shape[0]
    slot_total = n_expert * msg
    wide = 2 * width
    plane = n_expert * 2

    def cols(index, size):
        return pl.ds(pl.multiple_of(index * size, size), size)

    def band(e):
        return pl.ds(pl.multiple_of(e * msg, msg), msg)

    barrier = pltpu.get_barrier_semaphore()

    def greet(off, carry):
        other = lax.rem(e_me * 2 + c_me + off, plane)
        pl.semaphore_signal(
            barrier, inc=1, device_id=(other // 2, x_me * 2 + lax.rem(other, 2)), device_id_type=MESH
        )
        return carry

    lax.fori_loop(1, plane, greet, 0)
    pl.semaphore_signal(barrier, inc=1, device_id=far_peer, device_id_type=MESH)
    weight_copies = [
        pltpu.make_async_copy(src, dst, local_sem.at[i])
        for i, (src, dst) in enumerate(((wg_ref, wg), (wu_ref, wu), (wd_ref, wd)))
    ]
    for copy in weight_copies:
        copy.start()

    expert_ids = lax.broadcasted_iota(jnp.int32, (n_expert * el, row_count), 0)
    named = [expert_ids == routes_ref[k : k + 1, :] for k in range(TOPK)]
    either = sum(jnp.where(n, 1.0, 0.0) for n in named).astype(BF16)
    square = (row_count, row_count)
    row_ids, col_ids = lax.broadcasted_iota(jnp.int32, square, 0), lax.broadcasted_iota(jnp.int32, square, 1)
    earlier = jnp.where(row_ids < col_ids, 1.0, 0.0).astype(BF16)
    before = jnp.dot(either, earlier, preferred_element_type=F32)
    for k in range(TOPK):
        position = jnp.sum(jnp.where(named[k], before, 0.0), axis=0, keepdims=True)
        meta[0, k : k + 1, :] = routes_ref[k : k + 1, :].astype(F32) * CAP + position
        meta[0, TOPK + k : TOPK + k + 1, :] = gates_ref[k : k + 1, :]
    meta[0, 2 * TOPK :, :] = jnp.zeros((meta.shape[1] - 2 * TOPK, row_count), F32)
    def swap_copy(i, src, dst):
        return pltpu.make_async_remote_copy(
            src_ref=src, dst_ref=dst, send_sem=swap_sem.at[0, i], recv_sem=swap_sem.at[1, i],
            device_id=far_peer, device_id_type=MESH,
        )

    swaps = [
        swap_copy(0, tok_ref.at[:, cols(1 - x_me, wide)], halves.at[0]),
        swap_copy(1, cot_ref.at[:, cols(1 - x_me, wide)], halves.at[1]),
        swap_copy(2, meta.at[0], meta.at[1]),
    ]
    slot_ids = lax.broadcasted_iota(jnp.int32, (slot_total, row_count), 0).astype(F32)

    def placed(s):
        return [slot_ids == meta[s, k : k + 1, :] for k in range(TOPK)]

    def fill(s, tok, cot):
        picks = placed(s)
        selector = sum(jnp.where(p, 1.0, 0.0) for p in picks).astype(BF16)
        weight = sum(
            jnp.where(p, meta[s, TOPK + k : TOPK + k + 1, :], 0.0) for k, p in enumerate(picks)
        )
        weight = jnp.sum(weight, axis=1, keepdims=True)
        send[s, 0] = jnp.dot(selector, tok, preferred_element_type=F32).astype(BF16)
        send[s, 1] = (jnp.dot(selector, cot, preferred_element_type=F32) * weight).astype(BF16)

    def place(k, j):
        zh = lax.rem(zh_me + j // 2, n_zh)
        z = zh * 2 + lax.rem(zl_me + k % 2, 2)
        e = z * 2 + lax.rem(y_me + k // 2, 2)
        return e, zh, lax.rem(c_me + lax.rem(j, 2), 2)

    def source_dp(s, c):
        return (x_me if s == 0 else 1 - x_me) * 2 + c

    def in_copy(k, s, j):
        e, zh, c = place(k, j)
        pos = zh_me * n_dp + source_dp(s, c_me)
        return pltpu.make_async_remote_copy(
            src_ref=send.at[s, :, band(e), cols(c, width)],
            dst_ref=recv.at[k, pos],
            send_sem=in_send.at[k * per + zh * n_dp + c * 2 + s],
            recv_sem=in_recv.at[k * per + pos],
            device_id=(e, x_me * 2 + c),
            device_id_type=MESH,
        )

    def in_wait(k, s, j):
        e, zh, c = place(k, j)
        pos = zh * n_dp + source_dp(s, c)
        pltpu.make_async_remote_copy(
            src_ref=recv.at[k, pos],
            dst_ref=recv.at[k, pos],
            send_sem=in_send.at[k * per + zh * n_dp + c * 2 + s],
            recv_sem=in_recv.at[k * per + pos],
            device_id=(e, x_me * 2 + c),
            device_id_type=MESH,
        ).wait_recv()

    def out_copy(k, s, j):
        e, zh, c = place(k, j)
        return pltpu.make_async_remote_copy(
            src_ref=ret_send.at[k, zh * n_dp + source_dp(s, c)],
            dst_ref=ret.at[s, :, band(e_me), cols(c_me, width)],
            send_sem=out_send.at[k * per + zh * n_dp + c * 2 + s],
            recv_sem=out_recv.at[k * per + zh_me * n_dp + c_me * 2 + s],
            device_id=(e, x_me * 2 + c),
            device_id_type=MESH,
        )

    def out_wait(k, s, j):
        e, zh, c = place(k, j)
        spot = ret.at[s, :, band(e), cols(c, width)]
        pltpu.make_async_remote_copy(
            src_ref=spot,
            dst_ref=spot,
            send_sem=out_send.at[k * per + zh * n_dp + c * 2 + s],
            recv_sem=out_recv.at[k * per + zh * n_dp + c * 2 + s],
            device_id=(e, x_me * 2 + c),
            device_id_type=MESH,
        ).wait_recv()

    def each(k, body):
        count = n_zh * 2

        def step(j, carry):
            body(j)
            return carry

        lax.fori_loop(1 if k == 0 else 0, count, step, 0)

    def own_in(s):
        return pltpu.make_async_copy(
            send.at[s, :, band(e_me), cols(c_me, width)],
            recv.at[0, zh_me * n_dp + source_dp(s, c_me)],
            local_sem.at[3 + s],
        )

    def own_out(s):
        return pltpu.make_async_copy(
            ret_send.at[0, zh_me * n_dp + source_dp(s, c_me)],
            ret.at[s, :, band(e_me), cols(c_me, width)],
            local_sem.at[3 + s],
        )

    def send_chunk(k, s):
        each(k, lambda j: in_copy(k, s, j).start())
        if k == 0:
            own_in(s).start()

    fill(0, tok_ref[:, cols(x_me, wide)], cot_ref[:, cols(x_me, wide)])
    pl.semaphore_wait(barrier, plane)
    for copy in swaps:
        copy.start()
    send_chunk(0, 0)
    send_chunk(1, 0)
    for copy in swaps:
        copy.wait_recv()
    fill(1, halves[0], halves[1])
    for k, s in ((0, 1), (1, 1), (2, 0), (2, 1), (3, 0), (3, 1)):
        send_chunk(k, s)
    for copy in weight_copies:
        copy.wait()

    def pair_copy(k, src, dst, peer, stage):
        i = stage * 4 + k
        return pltpu.make_async_remote_copy(
            src_ref=src, dst_ref=dst, send_sem=pair_sem.at[0, i], recv_sem=pair_sem.at[1, i],
            device_id=peer, device_id_type=MESH,
        )

    def span(k):
        return pl.ds(k * part, part)

    mine = pl.ds(c_me * half, half)
    core_copy = [pair_copy(k, psend.at[k], crecv.at[k], core_peer, 0) for k in range(4)]
    far_copy = [pair_copy(k, xsend.at[k], xrecv.at[k], far_peer, 1) for k in range(4)]
    hid_copy = [
        pair_copy(k, hid.at[mine, span(k)], hid.at[mine, span(k)], core_peer, 2) for k in range(4)
    ]

    def partial(k, e, col):
        if col == 2:
            return jnp.dot(rows[e, span(k), width:], wd[e], preferred_element_type=F32)
        return jnp.dot(rows[e, span(k), :width], (wg, wu)[col][e], preferred_element_type=F32)

    def first_stage(k):
        for s in range(2):
            if k == 0:
                own_in(s).wait()
            each(k, lambda j, s=s: in_wait(k, s, j))
        for t in range(2):
            block = recv[k, :, t].reshape(per * msg, width)
            moved = jnp.dot(perm_ref[...], block, preferred_element_type=F32).astype(BF16)
            rows[:, k * part : (k + 1) * part, t * width : (t + 1) * width] = moved.reshape(
                el, part, width
            )

        def other(j, carry):
            for col in range(3):
                psend[k, j, :, col * ff : (col + 1) * ff] = partial(
                    k, (1 - c_me) * half + j, col
                ).astype(BF16)
            return carry

        lax.fori_loop(0, half, other, 0, unroll=True)
        core_copy[k].start()

        def own(j, carry):
            for col in range(3):
                pown[k, j, :, col * ff : (col + 1) * ff] = partial(k, c_me * half + j, col)
            return carry

        lax.fori_loop(0, half, own, 0, unroll=True)

    def chip_sum(k):
        core_copy[k].wait_recv()

        def body(j, carry):
            s = pown[k, j] + crecv[k, j].astype(F32)
            pown[k, j] = s
            xsend[k, j] = s.astype(BF16)
            return carry

        lax.fori_loop(0, half, body, 0)
        far_copy[k].start()

    def middle(k):
        far_copy[k].wait_recv()

        def body(j, carry):
            s = pown[k, j] + xrecv[k, j].astype(F32)
            gate_pre, up_pre, hidden_grad = s[:, :ff], s[:, ff : 2 * ff], s[:, 2 * ff :]
            sig = jax.nn.sigmoid(gate_pre)
            act = gate_pre * sig
            e = c_me * half + j
            hid[e, span(k), :ff] = (act * up_pre).astype(BF16)
            hid[e, span(k), ff : 2 * ff] = (
                hidden_grad * up_pre * sig * (1.0 + gate_pre * (1.0 - sig))
            ).astype(BF16)
            hid[e, span(k), 2 * ff :] = (hidden_grad * act).astype(BF16)
            return carry

        lax.fori_loop(0, half, body, 0)
        hid_copy[k].start()

    last = (((1,), (1,)), ((), ()))
    first = (((0,), (0,)), ((), ()))

    def last_stage(k):
        def body(j, carry, base):
            e = base + j
            h = hid[e, span(k)]
            pre_ret[0, e] = lax.dot_general(
                h[:, :ff], wd[e], last, preferred_element_type=F32
            ).astype(BF16)
            pre_ret[1, e] = (
                lax.dot_general(h[:, ff : 2 * ff], wg[e], last, preferred_element_type=F32)
                + lax.dot_general(h[:, 2 * ff :], wu[e], last, preferred_element_type=F32)
            ).astype(BF16)
            return carry

        lax.fori_loop(0, half, functools.partial(body, base=c_me * half), 0, unroll=True)
        hid_copy[k].wait_recv()
        lax.fori_loop(0, half, functools.partial(body, base=(1 - c_me) * half), 0, unroll=True)
        for t in range(2):
            block = pre_ret[t].reshape(el * part, width)
            moved = jnp.dot(back_ref[...], block, preferred_element_type=F32).astype(BF16)
            ret_send[k, :, t] = moved.reshape(per, msg, width)
        for s in (1, 0):
            each(k, lambda j, s=s: out_copy(k, s, j).start())
            if k == 0:
                own_out(s).start()

    first_stage(0)
    chip_sum(0)
    first_stage(1)
    chip_sum(1)
    first_stage(2)
    chip_sum(2)
    middle(0)
    last_stage(0)
    first_stage(3)
    chip_sum(3)
    for k in range(1, 4):
        middle(k)
        last_stage(k)

    def grads(e, carry):
        tok, grad = rows[e, :, :width], rows[e, :, width:]
        h = hid[e]
        dg[e] = lax.dot_general(
            tok, h[:, ff : 2 * ff], first, preferred_element_type=F32
        ).astype(BF16)
        du[e] = lax.dot_general(tok, h[:, 2 * ff :], first, preferred_element_type=F32).astype(BF16)
        dd[e] = lax.dot_general(grad, h[:, :ff], first, preferred_element_type=F32).astype(BF16)
        return carry

    lax.fori_loop(0, half, grads, 0)

    def combine(s):
        picks = [jnp.where(p, 1.0, 0.0) for p in placed(s)]
        out = 0.0
        for k in range(TOPK):
            gate = jnp.sum(
                jnp.where(row_ids == col_ids, meta[s, TOPK + k : TOPK + k + 1, :], 0.0),
                axis=1,
                keepdims=True,
            )
            picked = lax.dot_general(
                picks[k].astype(BF16), ret[s, 0], first, preferred_element_type=F32
            )
            out = out + gate * picked
        grad = lax.dot_general(
            sum(picks).astype(BF16), ret[s, 1], first, preferred_element_type=F32
        )
        return out.astype(BF16), grad.astype(BF16)

    fin_copy = [swap_copy(3 + i, fin_send.at[i], fin_recv.at[i]) for i in range(2)]
    for s in (1, 0):
        own_out(s).wait()
        for k in range(4):
            each(k, lambda j, k=k, s=s: out_wait(k, s, j))
        out, grad = combine(s)
        if s == 1:
            fin_send[0] = out
            fin_send[1] = grad
            for copy in fin_copy:
                copy.start()
            lax.fori_loop(half, el, grads, 0)
        else:
            layer_ref[:, cols(x_me, wide)] = out
            igrad_ref[:, cols(x_me, wide)] = grad
    for copy in swaps:
        copy.wait_send()
    for k in range(4):
        for s in range(2):
            each(k, lambda j, k=k, s=s: in_copy(k, s, j).wait_send())
            each(k, lambda j, k=k, s=s: out_copy(k, s, j).wait_send())
        core_copy[k].wait_send()
        far_copy[k].wait_send()
        hid_copy[k].wait_send()

    for copy in fin_copy:
        copy.wait()
    layer_ref[:, cols(1 - x_me, wide)] = fin_recv[0]
    igrad_ref[:, cols(1 - x_me, wide)] = fin_recv[1]


def shards(tokens, routes, gate_values, cotangent, gating_weight, upward_weight, down_weight):
    n_expert, n_dp = lax.axis_size("expert"), lax.axis_size("dp")
    el, width, ff = gating_weight.shape
    row_count = tokens.shape[0]
    per = n_expert * n_dp // 4
    msg = el * CAP
    part = per * CAP
    slots = 4 * part
    half = el // 2
    wide = 3 * ff
    spot = np.arange(per * msg)
    e, s, c = spot // part, spot % part // CAP, spot % CAP
    perm = np.zeros((per * msg, per * msg), np.float32)
    perm[spot, s * msg + e * CAP + c] = 1.0
    hbm = pl.BlockSpec(memory_space=pltpu.HBM)
    vmem = pl.BlockSpec(memory_space=pltpu.VMEM)
    weight_shape = gating_weight.shape
    layer_output, input_grad, dg, du, dd = pl.pallas_call(
        functools.partial(plane_kernel, n_expert, n_dp, el, width),
        out_shape=(
            jax.ShapeDtypeStruct(tokens.shape, BF16),
            jax.ShapeDtypeStruct(tokens.shape, BF16),
            jax.ShapeDtypeStruct(weight_shape, BF16),
            jax.ShapeDtypeStruct(weight_shape, BF16),
            jax.ShapeDtypeStruct(weight_shape, BF16),
        ),
        in_specs=[vmem] * 6 + [hbm] * 3,
        out_specs=[vmem] * 5,
        scratch_shapes=[
            pltpu.VMEM(weight_shape, BF16),
            pltpu.VMEM(weight_shape, BF16),
            pltpu.VMEM(weight_shape, BF16),
            pltpu.VMEM((2, row_count, 2 * width), BF16),
            pltpu.VMEM((2, 8, row_count), F32),
            pltpu.VMEM((2, 2, n_expert * msg, 2 * width), BF16),
            pltpu.VMEM((4, per, 2, msg, width), BF16),
            pltpu.VMEM((el, slots, 2 * width), BF16),
            pltpu.VMEM((4, half, part, wide), BF16),
            pltpu.VMEM((4, half, part, wide), F32),
            pltpu.VMEM((4, half, part, wide), BF16),
            pltpu.VMEM((4, half, part, wide), BF16),
            pltpu.VMEM((4, half, part, wide), BF16),
            pltpu.VMEM((el, slots, wide), BF16),
            pltpu.VMEM((2, el, part, width), BF16),
            pltpu.VMEM((4, per, 2, msg, width), BF16),
            pltpu.VMEM((2, 2, n_expert * msg, 2 * width), BF16),
            pltpu.VMEM((2, row_count, 2 * width), BF16),
            pltpu.VMEM((2, row_count, 2 * width), BF16),
            pltpu.SemaphoreType.DMA((4 * per,)),
            pltpu.SemaphoreType.DMA((4 * per,)),
            pltpu.SemaphoreType.DMA((4 * per,)),
            pltpu.SemaphoreType.DMA((4 * per,)),
            pltpu.SemaphoreType.DMA((2, 12)),
            pltpu.SemaphoreType.DMA((2, 5)),
            pltpu.SemaphoreType.DMA((5,)),
        ],
        compiler_params=pltpu.CompilerParams(
            collective_id=0, has_side_effects=True, vmem_limit_bytes=48 * 1024 * 1024
        ),
    )(
        tokens,
        cotangent,
        routes.T,
        gate_values.T,
        jnp.asarray(perm, BF16),
        jnp.asarray(perm.T, BF16),
        gating_weight,
        upward_weight,
        down_weight,
    )
    return (layer_output, input_grad, dg.astype(F32), du.astype(F32), dd.astype(F32))


def general_shards(tokens, routes, gate_values, cotangent, gating_weight, upward_weight, down_weight):
    expert_total = gating_weight.shape[0] * lax.axis_size("expert")
    row_count = tokens.shape[0]
    slot_total = expert_total * CAP
    flat_routes = routes.reshape(-1)
    onehot = (flat_routes[:, None] == jnp.arange(expert_total, dtype=jnp.int32)[None, :]).astype(
        jnp.int32
    )
    position = jnp.sum((jnp.cumsum(onehot, axis=0) - onehot) * onehot, axis=1)
    slot_index = flat_routes * CAP + position
    placed = (slot_index[:, None] == jnp.arange(slot_total, dtype=jnp.int32)[None, :]).astype(
        jnp.float32
    )
    placed = placed.reshape(row_count, TOPK, slot_total)
    selector = jnp.sum(placed, axis=1).astype(jnp.bfloat16)
    slot_gate = jnp.sum(placed * gate_values[:, :, None], axis=(0, 1))
    contract = (((0,), (0,)), ((), ()))
    send_rows = lax.dot_general(selector, tokens, contract, preferred_element_type=jnp.float32)
    send_rows = send_rows.astype(jnp.bfloat16).reshape(expert_total, CAP, -1)
    slot_cotangent = lax.dot_general(
        selector, cotangent, contract, preferred_element_type=jnp.float32
    )
    send_grads = (
        (slot_cotangent * slot_gate[:, None]).astype(jnp.bfloat16).reshape(expert_total, CAP, -1)
    )
    arrived, arrived_grad = (
        lax.all_to_all(send_rows, "expert", split_axis=0, concat_axis=1, tiled=True),
        lax.all_to_all(send_grads, "expert", split_axis=0, concat_axis=1, tiled=True),
    )
    gating, upward, lowering = (
        lax.all_gather(gating_weight, "dp", axis=1, tiled=True),
        lax.all_gather(upward_weight, "dp", axis=1, tiled=True),
        lax.all_gather(down_weight, "dp", axis=1, tiled=True),
    )
    gate_pre = jnp.einsum("erd,edf->erf", arrived, gating, preferred_element_type=jnp.float32)
    up_pre = jnp.einsum("erd,edf->erf", arrived, upward, preferred_element_type=jnp.float32)
    sigmoid_gate = jax.nn.sigmoid(gate_pre)
    activated = gate_pre * sigmoid_gate
    hidden = (activated * up_pre).astype(jnp.bfloat16)
    expert_out = jnp.einsum(
        "erf,edf->erd", hidden, lowering, preferred_element_type=jnp.float32
    ).astype(jnp.bfloat16)
    gating, upward, lowering = (
        lax.all_gather(gating_weight, "dp", axis=1, tiled=True),
        lax.all_gather(upward_weight, "dp", axis=1, tiled=True),
        lax.all_gather(down_weight, "dp", axis=1, tiled=True),
    )
    hidden_grad = jnp.einsum(
        "erd,edf->erf", arrived_grad, lowering, preferred_element_type=jnp.float32
    )
    gate_part = (
        hidden_grad * up_pre * sigmoid_gate * (1.0 + gate_pre * (1.0 - sigmoid_gate))
    ).astype(jnp.bfloat16)
    up_part = (hidden_grad * activated).astype(jnp.bfloat16)
    pair_grad = (
        jnp.einsum("erf,edf->erd", gate_part, gating, preferred_element_type=jnp.float32)
        + jnp.einsum("erf,edf->erd", up_part, upward, preferred_element_type=jnp.float32)
    ).astype(jnp.bfloat16)
    returned_out, returned_grad = (
        lax.all_to_all(expert_out, "expert", split_axis=1, concat_axis=0, tiled=True),
        lax.all_to_all(pair_grad, "expert", split_axis=1, concat_axis=0, tiled=True),
    )
    gating_term = jnp.einsum("erd,erf->edf", arrived, gate_part, preferred_element_type=jnp.float32)
    upward_term = jnp.einsum("erd,erf->edf", arrived, up_part, preferred_element_type=jnp.float32)
    down_term = jnp.einsum("erd,erf->edf", arrived_grad, hidden, preferred_element_type=jnp.float32)
    gating_grad, upward_grad, down_grad = (
        lax.psum_scatter(
            gating_term.astype(jnp.bfloat16), "dp", scatter_dimension=1, tiled=True
        ).astype(jnp.float32),
        lax.psum_scatter(
            upward_term.astype(jnp.bfloat16), "dp", scatter_dimension=1, tiled=True
        ).astype(jnp.float32),
        lax.psum_scatter(
            down_term.astype(jnp.bfloat16), "dp", scatter_dimension=1, tiled=True
        ).astype(jnp.float32),
    )
    returned_flat = returned_out.reshape(slot_total, -1)
    combined = jnp.zeros((row_count, returned_flat.shape[1]), jnp.float32)
    for choice_slot in range(TOPK):
        picker = placed[:, choice_slot, :].astype(jnp.bfloat16)
        picked = jnp.dot(picker, returned_flat, preferred_element_type=jnp.float32)
        combined = combined + gate_values[:, choice_slot][:, None] * picked
    layer_output = combined.astype(jnp.bfloat16)
    input_grad = jnp.dot(
        selector, returned_grad.reshape(slot_total, -1), preferred_element_type=jnp.float32
    ).astype(jnp.bfloat16)
    return (layer_output, input_grad, gating_grad, upward_grad, down_grad)


def solution(mesh):
    n_expert, n_dp = mesh.shape["expert"], mesh.shape["dp"]

    def program(*args):
        el = args[4].shape[0] // n_expert
        width = args[4].shape[1] // n_dp
        part = n_expert * n_dp // 4 * CAP
        fits = (
            n_dp == 4
            and n_expert % 4 == 0
            and el % 2 == 0
            and el * CAP % 16 == 0
            and part % 16 == 0
            and width % 128 == 0
            and args[4].shape[2] % 128 == 0
            and args[0].shape[0] // (n_expert * n_dp) % 128 == 0
        )
        return jax.shard_map(
            shards if fits else general_shards,
            mesh=mesh,
            in_specs=(
                P(("expert", "dp"), None),
                P(("expert", "dp"), None),
                P(("expert", "dp"), None),
                P(("expert", "dp"), None),
                P("expert", "dp", None),
                P("expert", "dp", None),
                P("expert", "dp", None),
            ),
            out_specs=(
                P(("expert", "dp"), None),
                P(("expert", "dp"), None),
                P("expert", "dp", None),
                P("expert", "dp", None),
                P("expert", "dp", None),
            ),
            check_vma=False,
        )(*args)

    return program
```

profile of v0, /device:TPU:0, one launch (start us, length us, event | category | flops | bytes accessed | tf_op | source)
XLA Modules:
  0.0 99.6 jit_solution(17929385370385211188)
XLA Ops:
  0.6 0.0 copy-start
  0.6 1.0 copy-done
  1.6 0.0 copy-start.1
  1.6 0.9 copy-done.1
  2.5 0.0 copy-start.2
  2.6 0.9 copy-done.2
  3.5 0.0 copy-start.3
  3.5 0.7 copy-done.3
  4.2 0.0 copy-start.4
  4.2 0.7 copy-done.4
  4.9 87.7 %shard_map.128 = (bf16[128,1024]{1,0:T(8,128)(2,1)S(1)}, bf16[128,1024]{1,0:T(8,128)(2,1)S(1)}, bf16[8,256,384]{2,1,0:T(8,128)(2,1)S(1)}, bf16[8,256,384]{2,1,0:T(8,128)(2,1)S(1)}, bf16[8,256,384]{2,1,0:T(8,128)(2,1)S(1)}) custom-call(bf16[128,1024]{1,0:T(8,128)(2,1)S(1)} %copy-done.1, bf16[128,1024]{1,0:T(8,128)(2,1)S(1)} %copy-done.2, ...), custom_call_target="tpu_custom_call" | custom-call | tf_op jit(solution)/shard_map/pallas_call | solution.py:405
  92.5 1.9 %convert_element_type.9 = f32[8,256,384]{2,1,0:T(8,128)} convert(bf16[8,256,384]{2,1,0:T(8,128)(2,1)S(1)} %get-tuple-element.12) | non-fusion elementwise | flops 786432 | bytes 4718592 | tf_op jit(solution)/shard_map/convert_element_type | solution.py:458
  94.4 1.9 %convert_element_type.10 = f32[8,256,384]{2,1,0:T(8,128)} convert(bf16[8,256,384]{2,1,0:T(8,128)(2,1)S(1)} %get-tuple-element.13) | non-fusion elementwise | flops 786432 | bytes 4718592 | tf_op jit(solution)/shard_map/convert_element_type | solution.py:458
  96.3 1.9 %convert_element_type.11 = f32[8,256,384]{2,1,0:T(8,128)} convert(bf16[8,256,384]{2,1,0:T(8,128)(2,1)S(1)} %get-tuple-element.14) | non-fusion elementwise | flops 786432 | bytes 4718592 | tf_op jit(solution)/shard_map/convert_element_type | solution.py:458
  98.2 0.7 copy.16
  98.9 0.7 copy.17
Async XLA Ops:
  0.6 1.0 copy-start
  1.6 0.9 copy-start.1
  2.5 0.9 copy-start.2
  3.5 0.7 copy-start.3
  4.2 0.7 copy-start.4
where the time goes:
time: 99.8 us; the launch traced here: 99.6 us
  Pallas kernels  87.7 us (88%)
  other arithmetic  5.64 us (6%)
  local copies, waits for them, and re-layouts  5.62 us (6%)
    pallas_call x1, Pallas kernels, shards(): pl.pallas_call(functools.partial(plane_kernel, n_expert, n_dp, el, width)...  87.7 us
    unnamed x12, local copies, waits for them, and re-layouts  5.62 us

commit v1 on v0

--- a/solution.py
+++ b/solution.py
@@ -16,8 +16,9 @@
 
 def plane_kernel(
     n_expert, n_dp, el, width,
-    tok_ref, cot_ref, routes_ref, gates_ref, perm_ref, back_ref, wg_ref, wu_ref, wd_ref,
+    tok_in, cot_in, routes_in, gates_in, perm_in, back_in, wg_ref, wu_ref, wd_ref,
     layer_ref, igrad_ref, dg, du, dd,
+    tok_ref, cot_ref, routes_ref, gates_ref, perm_ref, back_ref,
     wg, wu, wd, halves, meta, send, recv, rows, psend, pown, crecv, xsend, xrecv, hid,
     pre_ret, ret_send, ret, fin_send, fin_recv,
     in_send, in_recv, out_send, out_recv, pair_sem, swap_sem, local_sem,
@@ -46,6 +47,15 @@
     def band(e):
         return pl.ds(pl.multiple_of(e * msg, msg), msg)
 
+    input_copies = [
+        pltpu.make_async_copy(src, dst, local_sem.at[5 + i])
+        for i, (src, dst) in enumerate(
+            (
+                (routes_in, routes_ref), (gates_in, gates_ref), (tok_in, tok_ref), (cot_in, cot_ref),
+                (perm_in, perm_ref), (back_in, back_ref),
+            )
+        )
+    ]
     barrier = pltpu.get_barrier_semaphore()
 
     def greet(off, carry):
@@ -61,8 +71,12 @@
         pltpu.make_async_copy(src, dst, local_sem.at[i])
         for i, (src, dst) in enumerate(((wg_ref, wg), (wu_ref, wu), (wd_ref, wd)))
     ]
+    for copy in input_copies:
+        copy.start()
     for copy in weight_copies:
         copy.start()
+    for copy in input_copies[:4]:
+        copy.wait()
 
     expert_ids = lax.broadcasted_iota(jnp.int32, (n_expert * el, row_count), 0)
     named = [expert_ids == routes_ref[k : k + 1, :] for k in range(TOPK)]
@@ -197,6 +211,8 @@
     fill(1, halves[0], halves[1])
     for k, s in ((0, 1), (1, 1), (2, 0), (2, 1), (3, 0), (3, 1)):
         send_chunk(k, s)
+    for copy in input_copies[4:]:
+        copy.wait()
     for copy in weight_copies:
         copy.wait()
 
@@ -327,11 +343,9 @@
     def grads(e, carry):
         tok, grad = rows[e, :, :width], rows[e, :, width:]
         h = hid[e]
-        dg[e] = lax.dot_general(
-            tok, h[:, ff : 2 * ff], first, preferred_element_type=F32
-        ).astype(BF16)
-        du[e] = lax.dot_general(tok, h[:, 2 * ff :], first, preferred_element_type=F32).astype(BF16)
-        dd[e] = lax.dot_general(grad, h[:, :ff], first, preferred_element_type=F32).astype(BF16)
+        dg[e] = lax.dot_general(tok, h[:, ff : 2 * ff], first, preferred_element_type=F32)
+        du[e] = lax.dot_general(tok, h[:, 2 * ff :], first, preferred_element_type=F32)
+        dd[e] = lax.dot_general(grad, h[:, :ff], first, preferred_element_type=F32)
         return carry
 
     lax.fori_loop(0, half, grads, 0)
@@ -385,6 +399,20 @@
     igrad_ref[:, cols(1 - x_me, wide)] = fin_recv[1]
 
 
+def store_kernel(layer, igrad, dg, du, dd, layer_out, igrad_out, dg_out, du_out, dd_out, sem):
+    pairs = [
+        (src.at[e], dst.at[e])
+        for e in range(dg.shape[0])
+        for src, dst in ((dg, dg_out), (du, du_out), (dd, dd_out))
+    ]
+    pairs += [(layer, layer_out), (igrad, igrad_out)]
+    copies = [pltpu.make_async_copy(src, dst, sem.at[i]) for i, (src, dst) in enumerate(pairs)]
+    for copy in copies:
+        copy.start()
+    for copy in copies:
+        copy.wait()
+
+
 def shards(tokens, routes, gate_values, cotangent, gating_weight, upward_weight, down_weight):
     n_expert, n_dp = lax.axis_size("expert"), lax.axis_size("dp")
     el, width, ff = gating_weight.shape
@@ -405,15 +433,21 @@
     layer_output, input_grad, dg, du, dd = pl.pallas_call(
         functools.partial(plane_kernel, n_expert, n_dp, el, width),
         out_shape=(
-            jax.ShapeDtypeStruct(tokens.shape, BF16),
-            jax.ShapeDtypeStruct(tokens.shape, BF16),
-            jax.ShapeDtypeStruct(weight_shape, BF16),
-            jax.ShapeDtypeStruct(weight_shape, BF16),
-            jax.ShapeDtypeStruct(weight_shape, BF16),
+            pltpu.VMEM(tokens.shape, BF16),
+            pltpu.VMEM(tokens.shape, BF16),
+            pltpu.VMEM(weight_shape, F32),
+            pltpu.VMEM(weight_shape, F32),
+            pltpu.VMEM(weight_shape, F32),
         ),
-        in_specs=[vmem] * 6 + [hbm] * 3,
+        in_specs=[hbm] * 9,
         out_specs=[vmem] * 5,
         scratch_shapes=[
+            pltpu.VMEM(tokens.shape, BF16),
+            pltpu.VMEM(tokens.shape, BF16),
+            pltpu.VMEM((TOPK, row_count), jnp.int32),
+            pltpu.VMEM((TOPK, row_count), F32),
+            pltpu.VMEM(perm.shape, BF16),
+            pltpu.VMEM(perm.shape, BF16),
             pltpu.VMEM(weight_shape, BF16),
             pltpu.VMEM(weight_shape, BF16),
             pltpu.VMEM(weight_shape, BF16),
@@ -439,23 +473,36 @@
             pltpu.SemaphoreType.DMA((4 * per,)),
             pltpu.SemaphoreType.DMA((2, 12)),
             pltpu.SemaphoreType.DMA((2, 5)),
-            pltpu.SemaphoreType.DMA((5,)),
+            pltpu.SemaphoreType.DMA((11,)),
         ],
         compiler_params=pltpu.CompilerParams(
-            collective_id=0, has_side_effects=True, vmem_limit_bytes=48 * 1024 * 1024
+            collective_id=0, has_side_effects=True, vmem_limit_bytes=44 * 1024 * 1024
         ),
     )(
-        tokens,
-        cotangent,
-        routes.T,
-        gate_values.T,
-        jnp.asarray(perm, BF16),
-        jnp.asarray(perm.T, BF16),
-        gating_weight,
-        upward_weight,
-        down_weight,
-    )
-    return (layer_output, input_grad, dg.astype(F32), du.astype(F32), dd.astype(F32))
+        *(
+            pltpu.with_memory_space_constraint(a, pltpu.HBM)
+            for a in (
+                tokens,
+                cotangent,
+                routes.T,
+                gate_values.T,
+                jnp.asarray(perm, BF16),
+                jnp.asarray(perm.T, BF16),
+                gating_weight,
+                upward_weight,
+                down_weight,
+            )
+        )
+    )
+    results = (layer_output, input_grad, dg, du, dd)
+    return pl.pallas_call(
+        store_kernel,
+        out_shape=tuple(jax.ShapeDtypeStruct(r.shape, r.dtype) for r in results),
+        in_specs=[vmem] * 5,
+        out_specs=[hbm] * 5,
+        scratch_shapes=[pltpu.SemaphoreType.DMA((2 + 3 * el,))],
+        compiler_params=pltpu.CompilerParams(vmem_limit_bytes=16 * 1024 * 1024),
+    )(*results)
 
 
 def general_shards(tokens, routes, gate_values, cotangent, gating_weight, upward_weight, down_weight):

time: 99.8 us -> 92.7 us (0.929)
  other arithmetic: 5.64 us -> 0 us
  local copies, waits for them, and re-layouts: 5.62 us -> 0 us
  Pallas kernels: 87.7 us -> 91.9 us
    convert_element_type x3 -> x0, other arithmetic: 5.64 us -> none  [the longest x1 1.88 us: shards(): dg.astype(F32)]
    unnamed x12 -> x0, local copies, waits for them, and re-layouts: 5.62 us -> none
    pallas_call x0 -> x1, Pallas kernels: none -> 3.97 us  [shards(): pl.pallas_call(store_kernel, out_shape=tuple((jax.ShapeDtypeStruct(r.shap...]
where the time goes in v1:
time: 92.7 us; the launch traced here: 92.6 us
  Pallas kernels  91.9 us (99%)
    pallas_call x1, Pallas kernels, shards(): pl.pallas_call(functools.partial(plane_kernel, n_expert, n_dp, el, width)...  88 us
    pallas_call x1, Pallas kernels, shards(): pl.pallas_call(store_kernel, out_shape=tuple((jax.ShapeDtypeStruct(r.shap...  3.97 us

profile of v1, /device:TPU:0, one launch (start us, length us, event | category | flops | bytes accessed | tf_op | source)
XLA Modules:
  0.0 92.6 jit_solution(11799770954866017704)
XLA Ops:
  0.6 88.0 %shard_map.128 = (bf16[128,1024]{1,0:T(8,128)(2,1)S(1)}, bf16[128,1024]{1,0:T(8,128)(2,1)S(1)}, f32[8,256,384]{2,1,0:T(8,128)S(1)}, f32[8,256,384]{2,1,0:T(8,128)S(1)}, f32[8,256,384]{2,1,0:T(8,128)S(1)}) custom-call(bf16[128,1024]{1,0:T(8,128)(2,1)} %tok_in.1, bf16[128,1024]{1,0:T(8,128)(2,1)} %cot_in.1, s32[2,128]{1,0:T(2,128)} %bitcast.2, ...), custom_call_target="tpu_custom_call" | custom-call | tf_op jit(solution)/shard_map/pallas_call | solution.py:433
  88.6 4.0 %shard_map.129 = (bf16[128,1024]{1,0:T(8,128)(2,1)}, bf16[128,1024]{1,0:T(8,128)(2,1)}, f32[8,256,384]{2,1,0:T(8,128)}, f32[8,256,384]{2,1,0:T(8,128)}, f32[8,256,384]{2,1,0:T(8,128)}) custom-call(bf16[128,1024]{1,0:T(8,128)(2,1)S(1)} %get-tuple-element.10.layer, bf16[128,1024]{1,0:T(8,128)(2,1)S(1)} %get-tuple-element.11.igrad, ...), custom_call_target="tpu_custom_call" | custom-call | tf_op jit(solution)/shard_map/pallas_call | solution.py:498

commit v2 on v1

--- a/solution.py
+++ b/solution.py
@@ -12,6 +12,9 @@
 MESH = pl.DeviceIdType.MESH
 F32 = jnp.float32
 BF16 = jnp.bfloat16
+GROUPS = (((0, 0, 0), (1, 0, 0)), ((0, 1, 0), (1, 1, 0)), ((0, 0, 1), (1, 0, 1)), ((0, 1, 1), (1, 1, 1)))
+RETURNS = (((0, 1, 1), (0, 0, 1), (0, 1, 0), (0, 0, 0)), ((1, 1, 1), (1, 0, 1), (1, 1, 0), (1, 0, 0)), ((2, 1, 1), (2, 0, 1), (2, 1, 0), (2, 0, 0)), ((3, 1, 1), (3, 0, 1), (3, 1, 0), (3, 0, 0)))
+STEPS = (('send', ((0, 0, 0), (0, 1, 0), (1, 0, 0), (1, 1, 0))), ('load', 0), ('swap', 0), ('send', ((0, 0, 1), (0, 1, 1), (1, 0, 1), (1, 1, 1))), ('rows', 0), ('chip', 0), ('send', ((2, 0, 0), (2, 1, 0), (2, 0, 1), (2, 1, 1))), ('rows', 1), ('send', ((3, 0, 0), (3, 1, 0), (3, 0, 1), (3, 1, 1))), ('chip', 1), ('act', 0), ('rows', 2), ('chip', 2), ('act', 1), ('rows', 3), ('chip', 3), ('act', 2), ('act', 3))
 
 
 def plane_kernel(
@@ -28,10 +31,9 @@
     z_me, y_me = e_me // 2, lax.rem(e_me, 2)
     zh_me, zl_me = z_me // 2, lax.rem(z_me, 2)
     x_me, c_me = d_me // 2, lax.rem(d_me, 2)
-    n_zh = n_expert // 4
     core_peer = (e_me, x_me * 2 + 1 - c_me)
     far_peer = (e_me, (1 - x_me) * 2 + c_me)
-    per = n_zh * n_dp
+    per = n_dp * len(GROUPS[0])
     msg = el * CAP
     part = per * CAP
     half = el // 2
@@ -116,105 +118,83 @@
         send[s, 0] = jnp.dot(selector, tok, preferred_element_type=F32).astype(BF16)
         send[s, 1] = (jnp.dot(selector, cot, preferred_element_type=F32) * weight).astype(BF16)
 
-    def place(k, j):
-        zh = lax.rem(zh_me + j // 2, n_zh)
-        z = zh * 2 + lax.rem(zl_me + k % 2, 2)
-        e = z * 2 + lax.rem(y_me + k // 2, 2)
-        return e, zh, lax.rem(c_me + lax.rem(j, 2), 2)
-
-    def source_dp(s, c):
-        return (x_me if s == 0 else 1 - x_me) * 2 + c
-
-    def in_copy(k, s, j):
-        e, zh, c = place(k, j)
-        pos = zh_me * n_dp + source_dp(s, c_me)
+    def place(g, i, j):
+        far, zl, y = GROUPS[g][i]
+        z = lax.rem(zh_me + far, 2) * 2 + lax.rem(zl_me + zl, 2)
+        return z * 2 + lax.rem(y_me + y, 2), lax.rem(c_me + j, 2)
+
+    def home(g, i, j):
+        return not any(GROUPS[g][i]) and j == 0
+
+    def spot(i, s, c):
+        return i * n_dp + (x_me if s == 0 else 1 - x_me) * 2 + c
+
+    def message(g, i, s, j, src, dst, sems):
+        e, c = place(g, i, j)
         return pltpu.make_async_remote_copy(
-            src_ref=send.at[s, :, band(e), cols(c, width)],
-            dst_ref=recv.at[k, pos],
-            send_sem=in_send.at[k * per + zh * n_dp + c * 2 + s],
-            recv_sem=in_recv.at[k * per + pos],
+            src_ref=src,
+            dst_ref=dst,
+            send_sem=sems[0].at[g * per + spot(i, s, c)],
+            recv_sem=sems[1].at[g * per + spot(i, s, c_me)],
             device_id=(e, x_me * 2 + c),
             device_id_type=MESH,
         )
 
-    def in_wait(k, s, j):
-        e, zh, c = place(k, j)
-        pos = zh * n_dp + source_dp(s, c)
-        pltpu.make_async_remote_copy(
-            src_ref=recv.at[k, pos],
-            dst_ref=recv.at[k, pos],
-            send_sem=in_send.at[k * per + zh * n_dp + c * 2 + s],
-            recv_sem=in_recv.at[k * per + pos],
+    def in_copy(g, i, s, j):
+        e, c = place(g, i, j)
+        src = send.at[s, :, band(e), cols(c, width)]
+        dst = recv.at[g, spot(i, s, c_me)]
+        if home(g, i, j):
+            return pltpu.make_async_copy(src, dst, local_sem.at[3 + s])
+        return message(g, i, s, j, src, dst, (in_send, in_recv))
+
+    def out_copy(g, i, s, j):
+        e, c = place(g, i, j)
+        src = ret_send.at[g, spot(i, s, c)]
+        dst = ret.at[s, :, band(e_me), cols(c_me, width)]
+        if home(g, i, j):
+            return pltpu.make_async_copy(src, dst, local_sem.at[3 + s])
+        return message(g, i, s, j, src, dst, (out_send, out_recv))
+
+    def arrival(g, i, s, j, place_in, sems):
+        e, c = place(g, i, j)
+        return pltpu.make_async_remote_copy(
+            src_ref=place_in,
+            dst_ref=place_in,
+            send_sem=sems[0].at[g * per + spot(i, s, c)],
+            recv_sem=sems[1].at[g * per + spot(i, s, c)],
             device_id=(e, x_me * 2 + c),
             device_id_type=MESH,
-        ).wait_recv()
-
-    def out_copy(k, s, j):
-        e, zh, c = place(k, j)
-        return pltpu.make_async_remote_copy(
-            src_ref=ret_send.at[k, zh * n_dp + source_dp(s, c)],
-            dst_ref=ret.at[s, :, band(e_me), cols(c_me, width)],
-            send_sem=out_send.at[k * per + zh * n_dp + c * 2 + s],
-            recv_sem=out_recv.at[k * per + zh_me * n_dp + c_me * 2 + s],
-            device_id=(e, x_me * 2 + c),
-            device_id_type=MESH,
-        )
-
-    def out_wait(k, s, j):
-        e, zh, c = place(k, j)
-        spot = ret.at[s, :, band(e), cols(c, width)]
-        pltpu.make_async_remote_copy(
-            src_ref=spot,
-            dst_ref=spot,
-            send_sem=out_send.at[k * per + zh * n_dp + c * 2 + s],
-            recv_sem=out_recv.at[k * per + zh * n_dp + c * 2 + s],
-            device_id=(e, x_me * 2 + c),
-            device_id_type=MESH,
-        ).wait_recv()
-
-    def each(k, body):
-        count = n_zh * 2
-
-        def step(j, carry):
-            body(j)
-            return carry
-
-        lax.fori_loop(1 if k == 0 else 0, count, step, 0)
-
-    def own_in(s):
-        return pltpu.make_async_copy(
-            send.at[s, :, band(e_me), cols(c_me, width)],
-            recv.at[0, zh_me * n_dp + source_dp(s, c_me)],
-            local_sem.at[3 + s],
-        )
-
-    def own_out(s):
-        return pltpu.make_async_copy(
-            ret_send.at[0, zh_me * n_dp + source_dp(s, c_me)],
-            ret.at[s, :, band(e_me), cols(c_me, width)],
-            local_sem.at[3 + s],
-        )
-
-    def send_chunk(k, s):
-        each(k, lambda j: in_copy(k, s, j).start())
-        if k == 0:
-            own_in(s).start()
+        )
+
+    def in_wait(g, i, s):
+        for j in range(2):
+            if home(g, i, j):
+                in_copy(g, i, s, j).wait()
+            else:
+                c = place(g, i, j)[1]
+                arrival(g, i, s, j, recv.at[g, spot(i, s, c)], (in_send, in_recv)).wait_recv()
+
+    def out_wait(g, i, s):
+        for j in range(2):
+            if home(g, i, j):
+                out_copy(g, i, s, j).wait()
+            else:
+                e, c = place(g, i, j)
+                landed = ret.at[s, :, band(e), cols(c, width)]
+                arrival(g, i, s, j, landed, (out_send, out_recv)).wait_recv()
+
+    members = [(g, i) for g, group in enumerate(GROUPS) for i in range(len(group))]
+
+    def send_out(messages):
+        for g, i, s in messages:
+            for j in (1, 0):
+                in_copy(g, i, s, j).start()
 
     fill(0, tok_ref[:, cols(x_me, wide)], cot_ref[:, cols(x_me, wide)])
     pl.semaphore_wait(barrier, plane)
     for copy in swaps:
         copy.start()
-    send_chunk(0, 0)
-    send_chunk(1, 0)
-    for copy in swaps:
-        copy.wait_recv()
-    fill(1, halves[0], halves[1])
-    for k, s in ((0, 1), (1, 1), (2, 0), (2, 1), (3, 0), (3, 1)):
-        send_chunk(k, s)
-    for copy in input_copies[4:]:
-        copy.wait()
-    for copy in weight_copies:
-        copy.wait()
 
     def pair_copy(k, src, dst, peer, stage):
         i = stage * 4 + k
@@ -240,9 +220,8 @@
 
     def first_stage(k):
         for s in range(2):
-            if k == 0:
-                own_in(s).wait()
-            each(k, lambda j, s=s: in_wait(k, s, j))
+            for i in range(len(GROUPS[k])):
+                in_wait(k, i, s)
         for t in range(2):
             block = recv[k, :, t].reshape(per * msg, width)
             moved = jnp.dot(perm_ref[...], block, preferred_element_type=F32).astype(BF16)
@@ -321,24 +300,28 @@
             block = pre_ret[t].reshape(el * part, width)
             moved = jnp.dot(back_ref[...], block, preferred_element_type=F32).astype(BF16)
             ret_send[k, :, t] = moved.reshape(per, msg, width)
-        for s in (1, 0):
-            each(k, lambda j, s=s: out_copy(k, s, j).start())
-            if k == 0:
-                own_out(s).start()
-
-    first_stage(0)
-    chip_sum(0)
-    first_stage(1)
-    chip_sum(1)
-    first_stage(2)
-    chip_sum(2)
-    middle(0)
-    last_stage(0)
-    first_stage(3)
-    chip_sum(3)
-    for k in range(1, 4):
+        for g, i, s in RETURNS[k]:
+            for j in (1, 0):
+                out_copy(g, i, s, j).start()
+
+    def load(_):
+        for copy in input_copies[4:]:
+            copy.wait()
+        for copy in weight_copies:
+            copy.wait()
+
+    def swap_in(_):
+        for copy in swaps:
+            copy.wait_recv()
+        fill(1, halves[0], halves[1])
+
+    def act(k):
         middle(k)
         last_stage(k)
+
+    work = dict(send=send_out, load=load, rows=first_stage, swap=swap_in, chip=chip_sum, act=act)
+    for step, k in STEPS:
+        work[step](k)
 
     def grads(e, carry):
         tok, grad = rows[e, :, :width], rows[e, :, width:]
@@ -370,9 +353,8 @@
 
     fin_copy = [swap_copy(3 + i, fin_send.at[i], fin_recv.at[i]) for i in range(2)]
     for s in (1, 0):
-        own_out(s).wait()
-        for k in range(4):
-            each(k, lambda j, k=k, s=s: out_wait(k, s, j))
+        for g, i in members:
+            out_wait(g, i, s)
         out, grad = combine(s)
         if s == 1:
             fin_send[0] = out
@@ -386,9 +368,12 @@
     for copy in swaps:
         copy.wait_send()
     for k in range(4):
-        for s in range(2):
-            each(k, lambda j, k=k, s=s: in_copy(k, s, j).wait_send())
-            each(k, lambda j, k=k, s=s: out_copy(k, s, j).wait_send())
+        for i in range(len(GROUPS[k])):
+            for s in range(2):
+                for j in range(2):
+                    if not home(k, i, j):
+                        in_copy(k, i, s, j).wait_send()
+                        out_copy(k, i, s, j).wait_send()
         core_copy[k].wait_send()
         far_copy[k].wait_send()
         hid_copy[k].wait_send()
@@ -603,7 +588,7 @@
         part = n_expert * n_dp // 4 * CAP
         fits = (
             n_dp == 4
-            and n_expert % 4 == 0
+            and n_expert == sum(map(len, GROUPS))
             and el % 2 == 0
             and el * CAP % 16 == 0
             and part % 16 == 0

time: 92.7 us -> 87.9 us (0.948); the launches traced: 92.6 us -> 86.5 us
  Pallas kernels: 91.9 us -> 85.9 us
    pallas_call x1, Pallas kernels: 88 us -> 81.9 us  [shards(): pl.pallas_call(functools.partial(plane_kernel, n_expert, n_dp, el, width)...]
where the time goes in v2:
time: 87.9 us; the launch traced here: 86.5 us
  Pallas kernels  85.9 us (98%)
    pallas_call x1, Pallas kernels, shards(): pl.pallas_call(functools.partial(plane_kernel, n_expert, n_dp, el, width)...  81.9 us
    pallas_call x1, Pallas kernels, shards(): pl.pallas_call(store_kernel, out_shape=tuple((jax.ShapeDtypeStruct(r.shap...  3.97 us

profile of v2, /device:TPU:0, one launch (start us, length us, event | category | flops | bytes accessed | tf_op | source)
XLA Modules:
  0.0 86.5 jit_solution(2885714153690450048)
XLA Ops:
  0.6 81.9 %shard_map.128 = (bf16[128,1024]{1,0:T(8,128)(2,1)S(1)}, bf16[128,1024]{1,0:T(8,128)(2,1)S(1)}, f32[8,256,384]{2,1,0:T(8,128)S(1)}, f32[8,256,384]{2,1,0:T(8,128)S(1)}, f32[8,256,384]{2,1,0:T(8,128)S(1)}) custom-call(bf16[128,1024]{1,0:T(8,128)(2,1)} %tok_in.1, bf16[128,1024]{1,0:T(8,128)(2,1)} %cot_in.1, s32[2,128]{1,0:T(2,128)} %bitcast.2, ...), custom_call_target="tpu_custom_call" | custom-call | tf_op jit(solution)/shard_map/pallas_call | solution.py:418
  82.6 4.0 %shard_map.129 = (bf16[128,1024]{1,0:T(8,128)(2,1)}, bf16[128,1024]{1,0:T(8,128)(2,1)}, f32[8,256,384]{2,1,0:T(8,128)}, f32[8,256,384]{2,1,0:T(8,128)}, f32[8,256,384]{2,1,0:T(8,128)}) custom-call(bf16[128,1024]{1,0:T(8,128)(2,1)S(1)} %get-tuple-element.10.layer, bf16[128,1024]{1,0:T(8,128)(2,1)S(1)} %get-tuple-element.11.igrad, ...), custom_call_target="tpu_custom_call" | custom-call | tf_op jit(solution)/shard_map/pallas_call | solution.py:483

commit v3 on v2

--- a/solution.py
+++ b/solution.py
@@ -14,7 +14,7 @@
 BF16 = jnp.bfloat16
 GROUPS = (((0, 0, 0), (1, 0, 0)), ((0, 1, 0), (1, 1, 0)), ((0, 0, 1), (1, 0, 1)), ((0, 1, 1), (1, 1, 1)))
 RETURNS = (((0, 1, 1), (0, 0, 1), (0, 1, 0), (0, 0, 0)), ((1, 1, 1), (1, 0, 1), (1, 1, 0), (1, 0, 0)), ((2, 1, 1), (2, 0, 1), (2, 1, 0), (2, 0, 0)), ((3, 1, 1), (3, 0, 1), (3, 1, 0), (3, 0, 0)))
-STEPS = (('send', ((0, 0, 0), (0, 1, 0), (1, 0, 0), (1, 1, 0))), ('load', 0), ('swap', 0), ('send', ((0, 0, 1), (0, 1, 1), (1, 0, 1), (1, 1, 1))), ('rows', 0), ('chip', 0), ('send', ((2, 0, 0), (2, 1, 0), (2, 0, 1), (2, 1, 1))), ('rows', 1), ('send', ((3, 0, 0), (3, 1, 0), (3, 0, 1), (3, 1, 1))), ('chip', 1), ('act', 0), ('rows', 2), ('chip', 2), ('act', 1), ('rows', 3), ('chip', 3), ('act', 2), ('act', 3))
+STEPS = (('cross', 0), ('send', ((0, 1, 0), (1, 1, 0), (0, 1, 1), (1, 1, 1), (0, 0, 0), (0, 0, 1), (1, 0, 0))), ('load', 0), ('swap', 0), ('send', ((1, 0, 1), (2, 1, 0), (2, 0, 0))), ('rows', 0), ('chip', 0), ('send', ((2, 1, 1), (2, 0, 1))), ('rows', 1), ('send', ((3, 1, 0), (3, 0, 0), (3, 1, 1), (3, 0, 1))), ('chip', 1), ('act', 0), ('rows', 2), ('chip', 2), ('act', 1), ('rows', 3), ('chip', 3), ('act', 2), ('act', 3))
 
 
 def plane_kernel(
@@ -22,7 +22,7 @@
     tok_in, cot_in, routes_in, gates_in, perm_in, back_in, wg_ref, wu_ref, wd_ref,
     layer_ref, igrad_ref, dg, du, dd,
     tok_ref, cot_ref, routes_ref, gates_ref, perm_ref, back_ref,
-    wg, wu, wd, halves, meta, send, recv, rows, psend, pown, crecv, xsend, xrecv, hid,
+    wg, wu, wd, halves, meta, direct, send, recv, rows, psend, pown, crecv, xsend, xrecv, hid,
     pre_ret, ret_send, ret, fin_send, fin_recv,
     in_send, in_recv, out_send, out_recv, pair_sem, swap_sem, local_sem,
 ):
@@ -37,6 +37,7 @@
     msg = el * CAP
     part = per * CAP
     half = el // 2
+    some = half // 2
     ff = wg.shape[2]
     row_count = tok_ref.shape[0]
     slot_total = n_expert * msg
@@ -58,6 +59,9 @@
             )
         )
     ]
+    other_half = 1 - zh_me
+    ends = [e_me] + [(other_half * 2 + lax.rem(zl_me + zl, 2)) * 2 + y_me for zl in range(2)]
+    kind = lax.rem(zh_me + zl_me, 2)
     barrier = pltpu.get_barrier_semaphore()
 
     def greet(off, carry):
@@ -68,7 +72,9 @@
         return carry
 
     lax.fori_loop(1, plane, greet, 0)
-    pl.semaphore_signal(barrier, inc=1, device_id=far_peer, device_id_type=MESH)
+    across = [(e, (1 - x_me) * 2 + c) for e in ends for c in range(2)]
+    for other in across:
+        pl.semaphore_signal(barrier, inc=1, device_id=other, device_id_type=MESH)
     weight_copies = [
         pltpu.make_async_copy(src, dst, local_sem.at[i])
         for i, (src, dst) in enumerate(((wg_ref, wg), (wu_ref, wu), (wd_ref, wd)))
@@ -123,38 +129,83 @@
         z = lax.rem(zh_me + far, 2) * 2 + lax.rem(zl_me + zl, 2)
         return z * 2 + lax.rem(y_me + y, 2), lax.rem(c_me + j, 2)
 
+    def source(g, i, j):
+        far, zl, y = GROUPS[g][i]
+        if not far or g > 1:
+            return place(g, i, j)
+        z = other_half * 2 + lax.rem(other_half + zl, 2)
+        return z * 2 + lax.rem(y_me + y, 2), lax.rem(c_me + j, 2)
+
+    def label(g, i):
+        far, zl, _ = GROUPS[g][i]
+        return kind if far and g < 2 else g
+
+    def sent_as(g, i):
+        far, zl, _ = GROUPS[g][i]
+        return lax.rem(other_half + zl + zl_me, 2) if far and g < 2 else g
+
     def home(g, i, j):
         return not any(GROUPS[g][i]) and j == 0
 
     def spot(i, s, c):
         return i * n_dp + (x_me if s == 0 else 1 - x_me) * 2 + c
 
-    def message(g, i, s, j, src, dst, sems):
-        e, c = place(g, i, j)
+    def fill_direct():
+        other = cols(1 - x_me, wide)
+        for i, e in enumerate(ends):
+            ids = (lax.broadcasted_iota(jnp.int32, (msg, row_count), 0) + e * msg).astype(F32)
+            picks = [ids == meta[0, k : k + 1, :] for k in range(TOPK)]
+            selector = sum(jnp.where(p, 1.0, 0.0) for p in picks).astype(BF16)
+            weight = sum(
+                jnp.where(p, meta[0, TOPK + k : TOPK + k + 1, :], 0.0) for k, p in enumerate(picks)
+            )
+            weight = jnp.sum(weight, axis=1, keepdims=True)
+            direct[i, 0] = jnp.dot(selector, tok_ref[:, other], preferred_element_type=F32).astype(BF16)
+            direct[i, 1] = (
+                jnp.dot(selector, cot_ref[:, other], preferred_element_type=F32) * weight
+            ).astype(BF16)
+
+    def message(where, at_me, there, src, dst, sems):
         return pltpu.make_async_remote_copy(
             src_ref=src,
             dst_ref=dst,
-            send_sem=sems[0].at[g * per + spot(i, s, c)],
-            recv_sem=sems[1].at[g * per + spot(i, s, c_me)],
-            device_id=(e, x_me * 2 + c),
+            send_sem=sems[0].at[at_me],
+            recv_sem=sems[1].at[there],
+            device_id=where,
             device_id_type=MESH,
         )
+
+    def is_direct(g, i, s):
+        return s == 1 and (g == 0 or (g == 1 and i == 1))
 
     def in_copy(g, i, s, j):
         e, c = place(g, i, j)
+        group = label(g, i)
+        at_me = g * per + spot(i, s, c)
+        if is_direct(g, i, s):
+            pos = spot(i, 0, c_me)
+            return message(
+                (e, (1 - x_me) * 2 + c), at_me, group * per + pos,
+                direct.at[i + g, :, :, cols(c, width)], recv.at[group, pos], (in_send, in_recv),
+            )
+        pos = spot(i, s, c_me)
         src = send.at[s, :, band(e), cols(c, width)]
-        dst = recv.at[g, spot(i, s, c_me)]
         if home(g, i, j):
-            return pltpu.make_async_copy(src, dst, local_sem.at[3 + s])
-        return message(g, i, s, j, src, dst, (in_send, in_recv))
+            return pltpu.make_async_copy(src, recv.at[g, pos], local_sem.at[3 + s])
+        return message(
+            (e, x_me * 2 + c), at_me, group * per + pos, src, recv.at[group, pos], (in_send, in_recv)
+        )
 
     def out_copy(g, i, s, j):
-        e, c = place(g, i, j)
+        e, c = source(g, i, j)
         src = ret_send.at[g, spot(i, s, c)]
         dst = ret.at[s, :, band(e_me), cols(c_me, width)]
         if home(g, i, j):
             return pltpu.make_async_copy(src, dst, local_sem.at[3 + s])
-        return message(g, i, s, j, src, dst, (out_send, out_recv))
+        return message(
+            (e, x_me * 2 + c), g * per + spot(i, s, c), sent_as(g, i) * per + spot(i, s, c_me),
+            src, dst, (out_send, out_recv),
+        )
 
     def arrival(g, i, s, j, place_in, sems):
         e, c = place(g, i, j)
@@ -169,7 +220,7 @@
 
     def in_wait(g, i, s):
         for j in range(2):
-            if home(g, i, j):
+            if home(g, i, j) and s == 0:
                 in_copy(g, i, s, j).wait()
             else:
                 c = place(g, i, j)[1]
@@ -186,18 +237,26 @@
 
     members = [(g, i) for g, group in enumerate(GROUPS) for i in range(len(group))]
 
+    left = set()
+
+    def await_left(messages):
+        for g, i, s in messages:
+            for j in range(2):
+                if not home(g, i, j) or s:
+                    in_copy(g, i, s, j).wait_send()
+            left.add((g, i, s))
+
     def send_out(messages):
         for g, i, s in messages:
             for j in (1, 0):
                 in_copy(g, i, s, j).start()
 
     fill(0, tok_ref[:, cols(x_me, wide)], cot_ref[:, cols(x_me, wide)])
-    pl.semaphore_wait(barrier, plane)
-    for copy in swaps:
-        copy.start()
+    fill_direct()
+    pl.semaphore_wait(barrier, plane - 1 + len(across))
 
     def pair_copy(k, src, dst, peer, stage):
-        i = stage * 4 + k
+        i = (stage * 4 + k[0]) * 2 + k[1]
         return pltpu.make_async_remote_copy(
             src_ref=src, dst_ref=dst, send_sem=pair_sem.at[0, i], recv_sem=pair_sem.at[1, i],
             device_id=peer, device_id_type=MESH,
@@ -206,12 +265,24 @@
     def span(k):
         return pl.ds(k * part, part)
 
-    mine = pl.ds(c_me * half, half)
-    core_copy = [pair_copy(k, psend.at[k], crecv.at[k], core_peer, 0) for k in range(4)]
-    far_copy = [pair_copy(k, xsend.at[k], xrecv.at[k], far_peer, 1) for k in range(4)]
-    hid_copy = [
-        pair_copy(k, hid.at[mine, span(k)], hid.at[mine, span(k)], core_peer, 2) for k in range(4)
-    ]
+    def few(h, base=0):
+        return pl.ds(base + h * some, some)
+
+    parts = [(k, h) for k in range(4) for h in range(2)]
+    core_copy = {
+        (k, h): pair_copy((k, h), psend.at[k, few(h)], crecv.at[k, few(h)], core_peer, 0)
+        for k, h in parts
+    }
+    far_copy = {
+        (k, h): pair_copy((k, h), xsend.at[k, few(h)], xrecv.at[k, few(h)], far_peer, 1)
+        for k, h in parts
+    }
+    hid_copy = {
+        (k, h): pair_copy(
+            (k, h), hid.at[few(h, c_me * half), span(k)], hid.at[few(h, c_me * half), span(k)], core_peer, 2
+        )
+        for k, h in parts
+    }
 
     def partial(k, e, col):
         if col == 2:
@@ -236,8 +307,9 @@
                 ).astype(BF16)
             return carry
 
-        lax.fori_loop(0, half, other, 0, unroll=True)
-        core_copy[k].start()
+        for h in range(2):
+            lax.fori_loop(h * some, (h + 1) * some, other, 0, unroll=True)
+            core_copy[k, h].start()
 
         def own(j, carry):
             for col in range(3):
@@ -247,19 +319,19 @@
         lax.fori_loop(0, half, own, 0, unroll=True)
 
     def chip_sum(k):
-        core_copy[k].wait_recv()
-
         def body(j, carry):
             s = pown[k, j] + crecv[k, j].astype(F32)
             pown[k, j] = s
             xsend[k, j] = s.astype(BF16)
             return carry
 
-        lax.fori_loop(0, half, body, 0)
-        far_copy[k].start()
-
-    def middle(k):
-        far_copy[k].wait_recv()
+        for h in range(2):
+            core_copy[k, h].wait_recv()
+            lax.fori_loop(h * some, (h + 1) * some, body, 0)
+            far_copy[k, h].start()
+
+    def middle(k, h):
+        far_copy[k, h].wait_recv()
 
         def body(j, carry):
             s = pown[k, j] + xrecv[k, j].astype(F32)
@@ -274,8 +346,8 @@
             hid[e, span(k), 2 * ff :] = (hidden_grad * act).astype(BF16)
             return carry
 
-        lax.fori_loop(0, half, body, 0)
-        hid_copy[k].start()
+        lax.fori_loop(h * some, (h + 1) * some, body, 0)
+        hid_copy[k, h].start()
 
     last = (((1,), (1,)), ((), ()))
     first = (((0,), (0,)), ((), ()))
@@ -293,9 +365,16 @@
             ).astype(BF16)
             return carry
 
-        lax.fori_loop(0, half, functools.partial(body, base=c_me * half), 0, unroll=True)
-        hid_copy[k].wait_recv()
-        lax.fori_loop(0, half, functools.partial(body, base=(1 - c_me) * half), 0, unroll=True)
+        for h in range(2):
+            middle(k, h)
+            lax.fori_loop(
+                h * some, (h + 1) * some, functools.partial(body, base=c_me * half), 0, unroll=True
+            )
+        for h in range(2):
+            hid_copy[k, h].wait_recv()
+            lax.fori_loop(
+                h * some, (h + 1) * some, functools.partial(body, base=(1 - c_me) * half), 0, unroll=True
+            )
         for t in range(2):
             block = pre_ret[t].reshape(el * part, width)
             moved = jnp.dot(back_ref[...], block, preferred_element_type=F32).astype(BF16)
@@ -310,16 +389,16 @@
         for copy in weight_copies:
             copy.wait()
 
+    def swap_out(_):
+        for copy in swaps:
+            copy.start()
+
     def swap_in(_):
         for copy in swaps:
             copy.wait_recv()
         fill(1, halves[0], halves[1])
 
-    def act(k):
-        middle(k)
-        last_stage(k)
-
-    work = dict(send=send_out, load=load, rows=first_stage, swap=swap_in, chip=chip_sum, act=act)
+    work = dict(send=send_out, left=await_left, load=load, rows=first_stage, cross=swap_out, swap=swap_in, chip=chip_sum, act=last_stage)
     for step, k in STEPS:
         work[step](k)
 
@@ -371,12 +450,14 @@
         for i in range(len(GROUPS[k])):
             for s in range(2):
                 for j in range(2):
+                    if (k, i, s) not in left and (s or not home(k, i, j)):
+                        in_copy(k, i, s, j).wait_send()
                     if not home(k, i, j):
-                        in_copy(k, i, s, j).wait_send()
                         out_copy(k, i, s, j).wait_send()
-        core_copy[k].wait_send()
-        far_copy[k].wait_send()
-        hid_copy[k].wait_send()
+        for h in range(2):
+            core_copy[k, h].wait_send()
+            far_copy[k, h].wait_send()
+            hid_copy[k, h].wait_send()
 
     for copy in fin_copy:
         copy.wait()
@@ -438,6 +519,7 @@
             pltpu.VMEM(weight_shape, BF16),
             pltpu.VMEM((2, row_count, 2 * width), BF16),
             pltpu.VMEM((2, 8, row_count), F32),
+            pltpu.VMEM((3, 2, msg, 2 * width), BF16),
             pltpu.VMEM((2, 2, n_expert * msg, 2 * width), BF16),
             pltpu.VMEM((4, per, 2, msg, width), BF16),
             pltpu.VMEM((el, slots, 2 * width), BF16),
@@ -456,7 +538,7 @@
             pltpu.SemaphoreType.DMA((4 * per,)),
             pltpu.SemaphoreType.DMA((4 * per,)),
             pltpu.SemaphoreType.DMA((4 * per,)),
-            pltpu.SemaphoreType.DMA((2, 12)),
+            pltpu.SemaphoreType.DMA((2, 24)),
             pltpu.SemaphoreType.DMA((2, 5)),
             pltpu.SemaphoreType.DMA((11,)),
         ],
@@ -589,7 +671,7 @@
         fits = (
             n_dp == 4
             and n_expert == sum(map(len, GROUPS))
-            and el % 2 == 0
+            and el % 4 == 0
             and el * CAP % 16 == 0
             and part % 16 == 0
             and width % 128 == 0

time: 87.9 us -> 86.1 us (0.980); the launches traced: 86.5 us -> 85.9 us
  no operation moved by 1% of the time
where the time goes in v3:
time: 86.1 us; the launch traced here: 85.9 us
  Pallas kernels  85.3 us (99%)
    pallas_call x1, Pallas kernels, shards(): pl.pallas_call(functools.partial(plane_kernel, n_expert, n_dp, el, width)...  81.3 us
    pallas_call x1, Pallas kernels, shards(): pl.pallas_call(store_kernel, out_shape=tuple((jax.ShapeDtypeStruct(r.shap...  3.97 us

profile of v3, /device:TPU:0, one launch (start us, length us, event | category | flops | bytes accessed | tf_op | source)
XLA Modules:
  0.0 85.9 jit_solution(17569650134745018421)
XLA Ops:
  0.6 81.3 %shard_map.128 = (bf16[128,1024]{1,0:T(8,128)(2,1)S(1)}, bf16[128,1024]{1,0:T(8,128)(2,1)S(1)}, f32[8,256,384]{2,1,0:T(8,128)S(1)}, f32[8,256,384]{2,1,0:T(8,128)S(1)}, f32[8,256,384]{2,1,0:T(8,128)S(1)}) custom-call(bf16[128,1024]{1,0:T(8,128)(2,1)} %tok_in.1, bf16[128,1024]{1,0:T(8,128)(2,1)} %cot_in.1, s32[2,128]{1,0:T(2,128)} %bitcast.2, ...), custom_call_target="tpu_custom_call" | custom-call | tf_op jit(solution)/shard_map/pallas_call | solution.py:499
  82.0 4.0 %shard_map.129 = (bf16[128,1024]{1,0:T(8,128)(2,1)}, bf16[128,1024]{1,0:T(8,128)(2,1)}, f32[8,256,384]{2,1,0:T(8,128)}, f32[8,256,384]{2,1,0:T(8,128)}, f32[8,256,384]{2,1,0:T(8,128)}) custom-call(bf16[128,1024]{1,0:T(8,128)(2,1)S(1)} %get-tuple-element.10.layer, bf16[128,1024]{1,0:T(8,128)(2,1)S(1)} %get-tuple-element.11.igrad, ...), custom_call_target="tpu_custom_call" | custom-call | tf_op jit(solution)/shard_map/pallas_call | solution.py:565

commit v4 on v3

--- a/solution.py
+++ b/solution.py
@@ -466,12 +466,8 @@
 
 
 def store_kernel(layer, igrad, dg, du, dd, layer_out, igrad_out, dg_out, du_out, dd_out, sem):
-    pairs = [
-        (src.at[e], dst.at[e])
-        for e in range(dg.shape[0])
-        for src, dst in ((dg, dg_out), (du, du_out), (dd, dd_out))
-    ]
-    pairs += [(layer, layer_out), (igrad, igrad_out)]
+    pairs = [(dg, dg_out), (du, du_out), (dd, dd_out)]
+    pairs = [(layer, layer_out), (igrad, igrad_out)] + pairs
     copies = [pltpu.make_async_copy(src, dst, sem.at[i]) for i, (src, dst) in enumerate(pairs)]
     for copy in copies:
         copy.start()
@@ -567,7 +563,7 @@
         out_shape=tuple(jax.ShapeDtypeStruct(r.shape, r.dtype) for r in results),
         in_specs=[vmem] * 5,
         out_specs=[hbm] * 5,
-        scratch_shapes=[pltpu.SemaphoreType.DMA((2 + 3 * el,))],
+        scratch_shapes=[pltpu.SemaphoreType.DMA((5,))],
         compiler_params=pltpu.CompilerParams(vmem_limit_bytes=16 * 1024 * 1024),
     )(*results)
 

time: 86.1 us -> 86.1 us (level)
  no operation moved by 1% of the time
where the time goes in v4:
time: 86.1 us; the launch traced here: 85.9 us
  Pallas kernels  85.3 us (99%)
    pallas_call x1, Pallas kernels, shards(): pl.pallas_call(functools.partial(plane_kernel, n_expert, n_dp, el, width)...  81.3 us
    pallas_call x1, Pallas kernels, shards(): pl.pallas_call(store_kernel, out_shape=tuple((jax.ShapeDtypeStruct(r.shap...  3.95 us

profile of v4, /device:TPU:0, one launch (start us, length us, event | category | flops | bytes accessed | tf_op | source)
XLA Modules:
  0.0 85.9 jit_solution(17521458383575620487)
XLA Ops:
  0.6 81.3 %shard_map.128 = (bf16[128,1024]{1,0:T(8,128)(2,1)S(1)}, bf16[128,1024]{1,0:T(8,128)(2,1)S(1)}, f32[8,256,384]{2,1,0:T(8,128)S(1)}, f32[8,256,384]{2,1,0:T(8,128)S(1)}, f32[8,256,384]{2,1,0:T(8,128)S(1)}) custom-call(bf16[128,1024]{1,0:T(8,128)(2,1)} %tok_in.1, bf16[128,1024]{1,0:T(8,128)(2,1)} %cot_in.1, s32[2,128]{1,0:T(2,128)} %bitcast.2, ...), custom_call_target="tpu_custom_call" | custom-call | tf_op jit(solution)/shard_map/pallas_call | solution.py:495
  82.0 4.0 %shard_map.129 = (bf16[128,1024]{1,0:T(8,128)(2,1)}, bf16[128,1024]{1,0:T(8,128)(2,1)}, f32[8,256,384]{2,1,0:T(8,128)}, f32[8,256,384]{2,1,0:T(8,128)}, f32[8,256,384]{2,1,0:T(8,128)}) custom-call(bf16[128,1024]{1,0:T(8,128)(2,1)S(1)} %get-tuple-element.10.layer, bf16[128,1024]{1,0:T(8,128)(2,1)S(1)} %get-tuple-element.11.igrad, ...), custom_call_target="tpu_custom_call" | custom-call | tf_op jit(solution)/shard_map/pallas_call | solution.py:561
